TPU v7x, 32 devices: a whole 2x2x4 slice. The times are simulated.
32 devices in a mesh: space: 4 (over y, core), mode: 8 (over z, x).
Axes of the slice: x: 2, y: 2, z: 4, core: 2. Of those that a mesh axis runs over, the one named last changes fastest.
Arguments:
- intensity: float32 [1024, 8, 64, 256], P('mode', None, 'space'), may hold values from 0.1 to 2
- dir_cos: float32 [3, 32], replicated, may hold values from -1 to 1, as said below
- velocity: float32 [32], replicated, may hold values from 0.2 to 1
- rate: float32 [32], replicated, may hold values from 0.05 to 2
- spectrum: float32 [32], replicated, may hold values from 0.2 to 2
- weight: float32 [32], replicated, may hold values from 0.25 to 1.75
- heat: float32 [64, 256], P('space'), may hold values from 0.5 to 4
- rough_cells: int32 [4096], P('space'), may hold values from 0 to 4095, as said below
- rough_count: int32 [4], P('space'), may hold values from 256 to 1024, as said below
- rough_map: int32 [4096, 16], P('space'), may hold values from 0 to 15
Outputs:
- intensity_new: float32 [1024, 8, 64, 256], P('mode', None, 'space')
- energy_new: float32 [8, 64, 256], P(None, 'space')
Inputs may be any that keep to these rules, and one draw needn't show every extreme that they name: `dir_cos`: even directions have a positive third cosine, and direction 2k+1 equals direction 2k with the third cosine negated; every direction has a third cosine of magnitude 0.3 or more. `rough_cells`: the entries of one index of space are distinct. `rough_count`: some index of space has all 1024 slots live.
All inputs are finite; a program needn't handle non-finite values.
Results may differ from a plain program's by a relative error of at most 0.0015.
Values sent between devices are 32-bit elements; how exact they have to be, the bound alone decides.
A program may use at most 128 MiB of HBM per device.

v0:
```python
import jax
import jax.numpy as jnp
from jax import lax
from jax.sharding import PartitionSpec as P

PAIRS = 1024


def extended(block, sides, width):
    for axis, dim in sides:
        count = lax.axis_size(axis)
        forward = [(i, i + 1) for i in range(count - 1)]
        backward = [(target, source) for source, target in forward]
        low = lax.ppermute(
            lax.slice_in_dim(block, block.shape[dim] - width, None, axis=dim), axis, forward
        )
        high = lax.ppermute(lax.slice_in_dim(block, 0, width, axis=dim), axis, backward)
        block = jnp.concatenate([low, block, high], axis=dim)
    return block


def squash(energy):
    return energy / (1.0 + 0.3 * jnp.abs(energy))


def per_device(
    intensity, dir_cos, velocity, rate, spectrum, weight, heat, rough_cells, rough_count, rough_map
):
    pairs_local = intensity.shape[0]
    modes = velocity.shape[0]
    planes_count, rows, width = (intensity.shape[1], intensity.shape[2], intensity.shape[3])
    dirs_local = pairs_local // modes
    half = dirs_local // 2
    position = lax.axis_index("mode")
    cos_local = lax.dynamic_slice_in_dim(dir_cos, position * dirs_local, dirs_local, 1)
    weight_local = lax.dynamic_slice_in_dim(weight, position * dirs_local, dirs_local, 0)
    field = intensity.reshape(dirs_local, modes, planes_count, rows, width)
    partial_value = jnp.einsum("s,smzxy->zxy", weight_local, field)
    energy = lax.psum(partial_value, "mode") / PAIRS
    equil = squash(energy)
    padded = extended(field, (("space", 3),), 1)
    ox = cos_local[0][:, None, None, None, None]
    oy = cos_local[1][:, None, None, None, None]
    speed = velocity[None, :, None, None, None]
    pady = jnp.pad(field, ((0, 0), (0, 0), (0, 0), (0, 0), (1, 1)))
    along = jnp.maximum(ox, 0.0) * (field - padded[:, :, :, :-2]) + jnp.minimum(ox, 0.0) * (
        padded[:, :, :, 2:] - field
    )
    across = jnp.maximum(oy, 0.0) * (field - pady[..., :-2]) + jnp.minimum(oy, 0.0) * (
        pady[..., 2:] - field
    )
    source = (rate * spectrum)[:, None, None, None] * equil[None]
    rhs = field + source[None] - speed * (along + across)
    diag = 1.0 + rate
    couple = velocity[None, :] * jnp.abs(cos_local[2])[:, None]
    cdown = couple[1::2][:, :, None, None]
    adown = diag[None, :, None, None] + cdown
    down_rhs = rhs[1::2]
    carry = spectrum[None, :, None, None] * heat[None, None]
    planes = [None] * planes_count
    for level in reversed(range(planes_count)):
        carry = (down_rhs[:, :, level] + cdown * carry) / adown
        planes[level] = carry
    down_new = jnp.stack(planes, axis=2)
    bottom = down_new[:, :, 0].reshape(half, modes, rows * width)
    slots = rough_cells.shape[0]
    live = jnp.arange(slots, dtype=jnp.int32) < rough_count[0]
    everything = lax.all_gather(bottom, "mode", axis=0, tiled=True)
    values = everything[:, :, rough_cells]
    targets = lax.dynamic_slice_in_dim(rough_map, position * half, half, 1)
    picked = jnp.take_along_axis(values.transpose(2, 0, 1), targets[:, :, None], axis=1).transpose(
        1, 2, 0
    )
    current = bottom[:, :, rough_cells]
    inflow = 0.9 * bottom.at[:, :, rough_cells].set(jnp.where(live[None, None, :], picked, current))
    carry = inflow.reshape(half, modes, rows, width)
    cup = couple[0::2][:, :, None, None]
    aup = diag[None, :, None, None] + cup
    up_rhs = rhs[0::2]
    planes = []
    for level in range(planes_count):
        carry = (up_rhs[:, :, level] + cup * carry) / aup
        planes.append(carry)
    up_new = jnp.stack(planes, axis=2)
    fresh = jnp.stack([up_new, down_new], axis=1).reshape(
        dirs_local, modes, planes_count, rows, width
    )
    energy_new = lax.psum(jnp.einsum("s,smzxy->zxy", weight_local, fresh), "mode") / PAIRS
    return (fresh.reshape(pairs_local, planes_count, rows, width), energy_new)


def solution(mesh):
    in_specs = (
        P("mode", None, "space", None),
        P(),
        P(),
        P(),
        P(),
        P(),
        P("space", None),
        P("space"),
        P("space"),
        P("space", None),
    )
    out_specs = (P("mode", None, "space", None), P(None, "space", None))
    return jax.shard_map(
        per_device, mesh=mesh, in_specs=in_specs, out_specs=out_specs, check_vma=False
    )
```

profile of v0, /device:TPU:0, one launch (start us, length us, event | category | flops | bytes accessed | tf_op | source)
XLA Modules:
  0.0 554.9 jit_solution(16689023233069573652)
XLA Ops:
  7.2 7.9 %bitcast_reduce_fusion = bf16[4,8,16,256]{3,2,1,0:T(8,128)(2,1)S(1)} fusion(f32[128,8,16,256]{3,2,1,0:T(8,128)} %param.10), kind=kLoop, calls=%fused_computation.96 | loop fusion | flops 4063232 | bytes 17039360 | tf_op jit(solution)/shard_map/s,smzxy->zxy/reduce_sum | solution.py:38
  16.3 8.0 %fusion.37 = (f32[4,32,8,1,256]{4,3,2,1,0:T(1,128)S(1)}, f32[4,32,8,1,256]{4,3,2,1,0:T(1,128)S(1)}) fusion(f32[4,32,8,16,256]{4,3,2,1,0:T(8,128)} %bitcast.67), kind=kLoop, calls=%fused_computation.99 | loop fusion | bytes 4194304 | tf_op jit(solution)/shard_map/slice | solution.py:15
  24.4 2.5 collective-permute-start
  30.6 59.0 %all-reduce.4.cloned.1.call-done = f32[8,16,256]{2,1,0:T(8,128)} async-done(((f32[8,16,256]{2,1,0:T(8,128)}), f32[8,16,256]{2,1,0:T(8,128)}) %all-reduce.4.cloned.1.call-update) | async-done | bytes 131088 | tf_op jit(solution)/shard_map/psum | solution.py:39
  92.3 2.3 copy.239
  94.6 34.3 %fusion.5 = f32[4,32,8,16,256]{4,3,2,1,0:T(8,128)} fusion(f32[4,32,8,16,256]{4,3,2,1,0:T(8,128)} %bitcast.68, f32[4,32,8,1,256]{4,3,2,1,0:T(1,128)S(1)} %copy.239, f32[4,32,8,1,256]{4,3,2,1,0:T(1,128)S(1)} %copy.237, f32[4]{0:T(128)S(1)} %get-tuple-element.31, f32[4]{0:T(128)S(1)} %get-tuple-element.33, f32[4]{0:T(128)S(1)} %get-tuple-element.30, ...), kind=kLoop, calls=%fused_computation.11 | loop fusion | flops 67108864 | bytes 39846080 | tf_op jit(solution)/shard_map/sub | solution.py:53
  128.9 9.2 %fusion.36 = (f32[2,32,8,16,256]{4,3,2,1,0:T(8,128)}, f32[2,32,8,16,256]{4,3,2,1,0:T(8,128)S(1)}) fusion(f32[4,32,8,16,256]{4,3,2,1,0:T(8,128)} %fusion.5), kind=kLoop, calls=%fused_computation.98 | loop fusion | bytes 33554432 | tf_op jit(solution)/shard_map/slice | solution.py:79
  140.1 3.0 fusion.38
  143.2 3.4 copy-done.2
  146.6 2.5 squeeze.36
  149.0 2.4 squeeze.37
  151.4 2.4 squeeze.38
  153.8 2.4 squeeze.39
  156.2 2.4 squeeze.40
  160.2 4.9 add_divide_fusion.7
  168.4 5.9 %copy.244 = f32[2,32,4096]{1,0,2:T(2,128)} copy(f32[2,32,4096]{2,1,0:T(8,128)} %add_divide_fusion.7) | data formatting | bytes 2097152 | tf_op jit(solution)/shard_map/div | solution.py:62
  174.3 5.7 %gather_fusion.1 = f32[1024,2,32]{2,1,0:T(2,128)S(1)} fusion(f32[2,32,4096]{1,0,2:T(2,128)} %copy.244, s32[1024]{0:T(1024)S(1)} %get-tuple-element.27), kind=kCustom, calls=%fused_computation.1 | custom fusion | bytes 528384 | tf_op jit(solution)/shard_map/gather | solution.py:74
  180.0 108.7 %all-gather.2.cloned.1.call-done = f32[16,32,4096]{2,1,0:T(8,128)} async-done(((f32[2,32,4096]{2,1,0:T(8,128)}), f32[16,32,4096]{2,1,0:T(8,128)}) %all-gather.2.cloned.1.call-update) | async-done | bytes 8388624 | tf_op jit(solution)/shard_map/all_gather | solution.py:68
  288.8 23.2 %copy.241 = f32[16,32,4096]{1,0,2:T(8,128)} copy(f32[16,32,4096]{2,1,0:T(8,128)} %all-gather.2.cloned.1.call-done) | data formatting | bytes 16777216 | tf_op jit(solution)/shard_map/all_gather | solution.py:68
  312.0 19.9 %gather_fusion = f32[1024,16,32]{2,1,0:T(8,128)} fusion(f32[16,32,4096]{1,0,2:T(8,128)} %copy.241, s32[1024]{0:T(1024)S(1)} %get-tuple-element.27), kind=kCustom, calls=%fused_computation | custom fusion | bytes 4198400 | tf_op jit(solution)/shard_map/gather | solution.py:69
  331.9 20.6 %gather_fusion.2 = f32[2048,32]{1,0:T(8,128)S(1)} fusion(f32[1024,16,32]{2,1,0:T(8,128)} %gather_fusion, s32[2048]{0:T(1024)S(1)} %reshape.137), kind=kCustom, calls=%fused_computation.2 | custom fusion | bytes 540672 | tf_op jit(solution)/shard_map/jit(take_along_axis)/gather | solution.py:71
  352.5 3.9 fusion.22
  356.4 93.8 %scatter_fusion = f32[2,32,4096]{1,0,2:T(2,128)} fusion(f32[2,32,4096]{1,0,2:T(2,128)} %copy.244, s32[1024]{0:T(1024)S(1)} %get-tuple-element.28, f32[1024,2,32]{2,1,0:T(2,128)S(1)} %fusion.22), kind=kCustom, calls=%fused_computation.3 | custom fusion | bytes 790528 | tf_op jit(solution)/shard_map/scatter | solution.py:75
  450.2 5.8 %broadcast_multiply_fusion = f32[2,32,4096]{1,0,2:T(2,128)} fusion(f32[2,32,4096]{1,0,2:T(2,128)} %scatter_fusion), kind=kLoop, calls=%fused_computation.22 | loop fusion | flops 262144 | bytes 2097152 | tf_op jit(solution)/shard_map/mul | solution.py:75
  456.0 3.6 copy.254
  459.6 1.6 constant_dynamic-update-slice_fusion.6
  461.3 1.9 constant_dynamic-update-slice_fusion.5
  463.2 1.6 constant_dynamic-update-slice_fusion.4
  464.8 1.9 constant_dynamic-update-slice_fusion.3
  470.2 6.9 %fusion.32 = (bf16[2,2,8,16,256]{4,3,2,1,0:T(8,128)(2,1)S(1)}, f32[2,2,32,8,16,256]{5,4,3,2,1,0:T(8,128)}) fusion(f32[2,1,32,8,16,256]{5,4,3,2,1,0:T(8,128)S(1)} %bitcast.76, f32[2,1,32,8,16,256]{5,4,3,2,1,0:T(8,128)S(1)} %bitcast.73), kind=kLoop, calls=%fused_computation.97 | loop fusion | flops 8257536 | bytes 33816576 | tf_op jit(solution)/shard_map/s,smzxy->zxy/reduce_sum | solution.py:88
  478.1 68.6 %all-reduce.6.cloned.1.call-done = f32[8,16,256]{2,1,0:T(8,128)} async-done(((f32[8,16,256]{2,1,0:T(8,128)}), f32[8,16,256]{2,1,0:T(8,128)}) %all-reduce.6.cloned.1.call-update) | async-done | bytes 131088 | tf_op jit(solution)/shard_map/psum | solution.py:88
  546.8 1.6 broadcast_multiply_fusion.4
  (78 shorter events, 18.3 us)
Async XLA Ops:
  7.2 22.2 %copy-start = (f32[3,32]{1,0:T(4,128)S(1)}, f32[3,32]{1,0:T(4,128)}, u32[]{:S(2)}) copy-start(f32[3,32]{1,0:T(4,128)} %param.11) | copy-start | bytes 1156
  7.2 82.4 %all-reduce.4.cloned.1.call-start = ((), (), s32[]{:S(2)}) async-start(), calls=%async_computation | async-start | bytes 262144 | tf_op jit(solution)/shard_map/psum | solution.py:39
  7.2 7.9 %copy-start.9 = (f32[32]{0:T(128)S(1)}, f32[32]{0:T(128)}, u32[]{:S(2)}) copy-start(f32[32]{0:T(128)} %param.15) | copy-start | bytes 388
  15.1 14.4 %copy-start.4 = (f32[16,256]{1,0:T(8,128)S(1)}, f32[16,256]{1,0:T(8,128)}, u32[]{:S(2)}) copy-start(f32[16,256]{1,0:T(8,128)} %param.16) | copy-start | bytes 49156
  15.1 14.4 %copy-start.7 = (f32[32]{0:T(128)S(1)}, f32[32]{0:T(128)}, u32[]{:S(2)}) copy-start(f32[32]{0:T(128)} %param.12) | copy-start | bytes 388
  15.1 14.4 %copy-start.5 = (f32[32]{0:T(128)S(1)}, f32[32]{0:T(128)}, u32[]{:S(2)}) copy-start(f32[32]{0:T(128)} %param.14) | copy-start | bytes 388
  15.1 15.3 %copy-start.8 = (f32[32]{0:T(128)S(1)}, f32[32]{0:T(128)}, u32[]{:S(2)}) copy-start(f32[32]{0:T(128)} %param.13) | copy-start | bytes 388
  16.2 272.6 %all-gather.2.cloned.1.call-start = ((), (), s32[]{:S(2)}) async-start(), calls=%async_computation.1 | async-start | bytes 9437184 | tf_op jit(solution)/shard_map/all_gather | solution.py:68
  24.4 66.8 %collective-permute-start = (f32[4,32,8,1,256]{4,2,3,1,0:T(8,128)S(1)}, f32[4,32,8,1,256]{4,2,3,1,0:T(8,128)S(1)}, u32[]{:S(2)}, u32[]{:S(2)}) collective-permute-start(f32[4,32,8,1,256]{4,2,3,1,0:T(8,128)S(1)} %copy.236), channel_id=1, source_target_pairs={{0,8},{8,16},{16,24},{1,9},{9,17},{17,25},{2,10},{10,18},{18,26},{... | collective-permute-start | bytes 3145736 | tf_op jit(solution)/shard_map/ppermute | solution.py:14
  27.9 64.4 %collective-permute-start.1 = (f32[4,32,8,1,256]{4,2,3,1,0:T(8,128)}, f32[4,32,8,1,256]{4,2,3,1,0:T(8,128)}, u32[]{:S(2)}, u32[]{:S(2)}) collective-permute-start(f32[4,32,8,1,256]{4,2,3,1,0:T(8,128)} %copy.238), channel_id=1, source_target_pairs={{8,0},{16,8},{24,16},{9,1},{17,9},{25,17},{10,2},{18,10},{26,18},{... | collective-permute-start | bytes 3145736 | tf_op jit(solution)/shard_map/ppermute | solution.py:17
  143.2 3.4 copy-start.2
  146.5 12.1 %copy-start.3 = (f32[2,32,1,16,256]{4,3,2,1,0:T(8,128)S(1)}, f32[2,32,1,16,256]{4,3,2,1,0:T(8,128)}, u32[]{:S(2)}) copy-start(f32[2,32,1,16,256]{4,3,2,1,0:T(8,128)} %get-tuple-element.21) | copy-start | bytes 3145732
  159.8 8.6 %copy-start.6 = (s32[1024]{0:T(1024)S(1)}, s32[1024]{0:T(1024)}, u32[]{:S(2)}) copy-start(s32[1024]{0:T(1024)} %param.17) | copy-start | bytes 12292
  165.0 381.7 %all-reduce.6.cloned.1.call-start = ((), (), s32[]{:S(2)}) async-start(), calls=%async_computation.2 | async-start | bytes 262144 | tf_op jit(solution)/shard_map/psum | solution.py:88
  459.6 7.1 %slice-start = ((s8[8388608]{0:T(1024)(128)(4,1)}), s8[4194304]{0:T(1024)(128)(4,1)S(1)}, s32[]{:S(2)}) async-start(s8[8388608]{0:T(1024)(128)(4,1)} %bitcast.69), calls=%async_computation.3 | async-start | bytes 8388608
  463.1 3.6 slice-start.1
  466.7 2.2 slice-start.2
  467.0 3.3 slice-start.3
  470.2 78.1 %copy-start.1 = (f32[3,32]{1,0:T(4,128)S(1)}, f32[3,32]{1,0:T(4,128)}, u32[]{:S(2)}) copy-start(f32[3,32]{1,0:T(4,128)} %param.11) | copy-start | bytes 1156
Sparse Core Ops, SparseCore 0:
  16.3 73.2 all-reduce.3
  165.2 123.5 all-gather.1
  478.3 68.4 all-reduce.5
where the time goes:
time: 558 us; the launch traced here: 555 us
  waiting for transfers between devices  236 us (42%)
  local copies, waits for them, and re-layouts  216 us (39%)
  other arithmetic  82.2 us (15%)
  between operations  14.8 us (3%)
    all_gather x1, waiting for transfers between devices, per_device(): everything = lax.all_gather(bottom, 'mode', axis=0, tiled=True)  109 us
    scatter x1, local copies, waits for them, and re-layouts, per_device(): bottom.at[:, :, rough_cells]  93.8 us
    psum x1, waiting for transfers between devices, per_device(): lax.psum(jnp.einsum('s,smzxy->zxy', weight_local, fresh), 'mode') / PAIRS  68.6 us
    psum x1, waiting for transfers between devices, per_device(): energy = lax.psum(partial_value, 'mode') / PAIRS  59 us
    sub x1, other arithmetic, per_device(): rhs = field + source[None] - speed * (along + across)  34.3 us
    all_gather x1, local copies, waits for them, and re-layouts, per_device(): everything = lax.all_gather(bottom, 'mode', axis=0, tiled=True)  23.2 us
    gather x3, local copies, waits for them, and re-layouts, per_device(): jnp.take_along_axis(values.transpose(2, 0, 1), targets[:, :, None], axis=1)  21.1 us
    gather x1, local copies, waits for them, and re-layouts, per_device(): values = everything[:, :, rough_cells]  19.9 us
  transfers between devices with their start and end apart: 5, of which 3 were waited for; matrix products, arithmetic and copies ran while one was open for 5% of the time, Pallas kernels for 0%

commit v1 on v0

--- a/solution.py
+++ b/solution.py
@@ -1,9 +1,18 @@
+import functools
 import jax
 import jax.numpy as jnp
 from jax import lax
 from jax.sharding import PartitionSpec as P
 
 PAIRS = 1024
+
+
+def patch_wrap(message, device_axis):
+    out_arr = lax.all_gather(message, device_axis)
+    return jnp.sum(out_arr, 0)
+
+
+make_counts = functools.partial(patch_wrap, device_axis="mode")
 
 
 def extended(block, sides, width):
@@ -85,7 +94,7 @@
     fresh = jnp.stack([up_new, down_new], axis=1).reshape(
         dirs_local, modes, planes_count, rows, width
     )
-    energy_new = lax.psum(jnp.einsum("s,smzxy->zxy", weight_local, fresh), "mode") / PAIRS
+    energy_new = make_counts(jnp.einsum("s,smzxy->zxy", weight_local, fresh)) / PAIRS
     return (fresh.reshape(pairs_local, planes_count, rows, width), energy_new)
 
 

time: 558 us -> 528 us (0.946)
  waiting for transfers between devices: 236 us -> 206 us
    psum x1 -> x0, waiting for transfers between devices: 68.6 us -> none  [per_device(): lax.psum(jnp.einsum('s,smzxy->zxy', weight_local, fresh), 'mode') / PAIRS]
    all_gather x0 -> x1, waiting for transfers between devices: none -> 38.4 us  [patch_wrap(): out_arr = lax.all_gather(message, device_axis)]
where the time goes in v1:
time: 528 us; the launch traced here: 525 us
  local copies, waits for them, and re-layouts  216 us (41%)
  waiting for transfers between devices  206 us (39%)
  other arithmetic  82.6 us (16%)
  between operations  14.8 us (3%)
    all_gather x1, waiting for transfers between devices, per_device(): everything = lax.all_gather(bottom, 'mode', axis=0, tiled=True)  109 us
    scatter x1, local copies, waits for them, and re-layouts, per_device(): bottom.at[:, :, rough_cells]  93.8 us
    psum x1, waiting for transfers between devices, per_device(): energy = lax.psum(partial_value, 'mode') / PAIRS  59 us
    all_gather x1, waiting for transfers between devices, patch_wrap(): out_arr = lax.all_gather(message, device_axis)  38.4 us
    sub x1, other arithmetic, per_device(): rhs = field + source[None] - speed * (along + across)  34.3 us
    all_gather x1, local copies, waits for them, and re-layouts, per_device(): everything = lax.all_gather(bottom, 'mode', axis=0, tiled=True)  23.2 us
    gather x3, local copies, waits for them, and re-layouts, per_device(): jnp.take_along_axis(values.transpose(2, 0, 1), targets[:, :, None], axis=1)  21.1 us
    gather x1, local copies, waits for them, and re-layouts, per_device(): values = everything[:, :, rough_cells]  19.9 us
  transfers between devices with their start and end apart: 5, of which 3 were waited for; matrix products, arithmetic and copies ran while one was open for 5% of the time, Pallas kernels for 0%

profile of v1, /device:TPU:0, one launch (start us, length us, event | category | flops | bytes accessed | tf_op | source)
XLA Modules:
  0.0 525.0 jit_solution(3384562506161626650)
XLA Ops:
  7.2 7.9 %bitcast_reduce_fusion = bf16[4,8,16,256]{3,2,1,0:T(8,128)(2,1)S(1)} fusion(f32[128,8,16,256]{3,2,1,0:T(8,128)} %param.10), kind=kLoop, calls=%fused_computation.96 | loop fusion | flops 4063232 | bytes 17039360 | tf_op jit(solution)/shard_map/s,smzxy->zxy/reduce_sum | solution.py:47
  16.3 8.0 %fusion.37 = (f32[4,32,8,1,256]{4,3,2,1,0:T(1,128)S(1)}, f32[4,32,8,1,256]{4,3,2,1,0:T(1,128)S(1)}) fusion(f32[4,32,8,16,256]{4,3,2,1,0:T(8,128)} %bitcast.68), kind=kLoop, calls=%fused_computation.99 | loop fusion | bytes 4194304 | tf_op jit(solution)/shard_map/slice | solution.py:24
  24.4 2.5 collective-permute-start
  27.9 1.5 collective-permute-start.1
  30.6 59.0 %all-reduce.3.cloned.1.call-done = f32[8,16,256]{2,1,0:T(8,128)} async-done(((f32[8,16,256]{2,1,0:T(8,128)}), f32[8,16,256]{2,1,0:T(8,128)}) %all-reduce.3.cloned.1.call-update) | async-done | bytes 131088 | tf_op jit(solution)/shard_map/psum | solution.py:48
  92.3 2.3 copy.239
  94.6 34.3 %fusion.5 = f32[4,32,8,16,256]{4,3,2,1,0:T(8,128)} fusion(f32[4,32,8,16,256]{4,3,2,1,0:T(8,128)} %bitcast.69, f32[4,32,8,1,256]{4,3,2,1,0:T(1,128)S(1)} %copy.239, f32[4,32,8,1,256]{4,3,2,1,0:T(1,128)S(1)} %copy.237, f32[4]{0:T(128)S(1)} %get-tuple-element.31, f32[4]{0:T(128)S(1)} %get-tuple-element.33, f32[4]{0:T(128)S(1)} %get-tuple-element.30, ...), kind=kLoop, calls=%fused_computation.11 | loop fusion | flops 67108864 | bytes 39846080 | tf_op jit(solution)/shard_map/sub | solution.py:62
  128.9 9.2 %fusion.36 = (f32[2,32,8,16,256]{4,3,2,1,0:T(8,128)}, f32[2,32,8,16,256]{4,3,2,1,0:T(8,128)S(1)}) fusion(f32[4,32,8,16,256]{4,3,2,1,0:T(8,128)} %fusion.5), kind=kLoop, calls=%fused_computation.98 | loop fusion | bytes 33554432 | tf_op jit(solution)/shard_map/slice | solution.py:88
  140.1 3.0 fusion.38
  143.2 3.4 copy-done.2
  146.6 2.5 squeeze.36
  149.0 2.4 squeeze.37
  151.4 2.4 squeeze.38
  153.8 2.4 squeeze.39
  156.2 2.4 squeeze.40
  160.2 4.9 add_divide_fusion.7
  168.4 5.9 %copy.244 = f32[2,32,4096]{1,0,2:T(2,128)} copy(f32[2,32,4096]{2,1,0:T(8,128)} %add_divide_fusion.7) | data formatting | bytes 2097152 | tf_op jit(solution)/shard_map/div | solution.py:71
  174.3 5.7 %gather_fusion.1 = f32[1024,2,32]{2,1,0:T(2,128)S(1)} fusion(f32[2,32,4096]{1,0,2:T(2,128)} %copy.244, s32[1024]{0:T(1024)S(1)} %get-tuple-element.27), kind=kCustom, calls=%fused_computation.1 | custom fusion | bytes 528384 | tf_op jit(solution)/shard_map/gather | solution.py:83
  180.0 108.7 %all-gather.4.cloned.1.call-done = f32[16,32,4096]{2,1,0:T(8,128)} async-done(((f32[2,32,4096]{2,1,0:T(8,128)}), f32[16,32,4096]{2,1,0:T(8,128)}) %all-gather.4.cloned.1.call-update) | async-done | bytes 8388624 | tf_op jit(solution)/shard_map/all_gather | solution.py:77
  288.8 23.2 %copy.241 = f32[16,32,4096]{1,0,2:T(8,128)} copy(f32[16,32,4096]{2,1,0:T(8,128)} %all-gather.4.cloned.1.call-done) | data formatting | bytes 16777216 | tf_op jit(solution)/shard_map/all_gather | solution.py:77
  312.0 19.9 %gather_fusion = f32[1024,16,32]{2,1,0:T(8,128)} fusion(f32[16,32,4096]{1,0,2:T(8,128)} %copy.241, s32[1024]{0:T(1024)S(1)} %get-tuple-element.27), kind=kCustom, calls=%fused_computation | custom fusion | bytes 4198400 | tf_op jit(solution)/shard_map/gather | solution.py:78
  331.9 20.6 %gather_fusion.2 = f32[2048,32]{1,0:T(8,128)S(1)} fusion(f32[1024,16,32]{2,1,0:T(8,128)} %gather_fusion, s32[2048]{0:T(1024)S(1)} %reshape.137), kind=kCustom, calls=%fused_computation.2 | custom fusion | bytes 540672 | tf_op jit(solution)/shard_map/jit(take_along_axis)/gather | solution.py:80
  352.5 3.9 fusion.22
  356.4 93.8 %scatter_fusion = f32[2,32,4096]{1,0,2:T(2,128)} fusion(f32[2,32,4096]{1,0,2:T(2,128)} %copy.244, s32[1024]{0:T(1024)S(1)} %get-tuple-element.28, f32[1024,2,32]{2,1,0:T(2,128)S(1)} %fusion.22), kind=kCustom, calls=%fused_computation.3 | custom fusion | bytes 790528 | tf_op jit(solution)/shard_map/scatter | solution.py:84
  450.2 5.8 %broadcast_multiply_fusion = f32[2,32,4096]{1,0,2:T(2,128)} fusion(f32[2,32,4096]{1,0,2:T(2,128)} %scatter_fusion), kind=kLoop, calls=%fused_computation.22 | loop fusion | flops 262144 | bytes 2097152 | tf_op jit(solution)/shard_map/mul | solution.py:84
  456.0 3.6 copy.254
  459.6 1.6 constant_dynamic-update-slice_fusion.6
  461.3 1.9 constant_dynamic-update-slice_fusion.5
  463.2 1.6 constant_dynamic-update-slice_fusion.4
  464.8 1.9 constant_dynamic-update-slice_fusion.3
  470.2 6.9 %fusion.32 = (bf16[2,2,8,16,256]{4,3,2,1,0:T(8,128)(2,1)S(1)}, f32[2,2,32,8,16,256]{5,4,3,2,1,0:T(8,128)}) fusion(f32[2,1,32,8,16,256]{5,4,3,2,1,0:T(8,128)S(1)} %bitcast.77, f32[2,1,32,8,16,256]{5,4,3,2,1,0:T(8,128)S(1)} %bitcast.74), kind=kLoop, calls=%fused_computation.97 | loop fusion | flops 8257536 | bytes 33816576 | tf_op jit(solution)/shard_map/s,smzxy->zxy/reduce_sum | solution.py:97
  478.1 38.4 %all-gather.6.cloned.1.call-done = f32[64,16,256]{2,1,0:T(8,128)} async-done(((f32[8,16,256]{2,1,0:T(8,128)}), f32[64,16,256]{2,1,0:T(8,128)}) %all-gather.6.cloned.1.call-update) | async-done | bytes 1048592 | tf_op jit(solution)/shard_map/all_gather | solution.py:11
  (79 shorter events, 18.8 us)
Async XLA Ops:
  7.2 22.2 %copy-start = (f32[3,32]{1,0:T(4,128)S(1)}, f32[3,32]{1,0:T(4,128)}, u32[]{:S(2)}) copy-start(f32[3,32]{1,0:T(4,128)} %param.11) | copy-start | bytes 1156
  7.2 82.4 %all-reduce.3.cloned.1.call-start = ((), (), s32[]{:S(2)}) async-start(), calls=%async_computation | async-start | bytes 262144 | tf_op jit(solution)/shard_map/psum | solution.py:48
  7.2 7.9 %copy-start.9 = (f32[32]{0:T(128)S(1)}, f32[32]{0:T(128)}, u32[]{:S(2)}) copy-start(f32[32]{0:T(128)} %param.15) | copy-start | bytes 388
  15.1 14.4 %copy-start.4 = (f32[16,256]{1,0:T(8,128)S(1)}, f32[16,256]{1,0:T(8,128)}, u32[]{:S(2)}) copy-start(f32[16,256]{1,0:T(8,128)} %param.16) | copy-start | bytes 49156
  15.1 14.4 %copy-start.7 = (f32[32]{0:T(128)S(1)}, f32[32]{0:T(128)}, u32[]{:S(2)}) copy-start(f32[32]{0:T(128)} %param.12) | copy-start | bytes 388
  15.1 14.4 %copy-start.5 = (f32[32]{0:T(128)S(1)}, f32[32]{0:T(128)}, u32[]{:S(2)}) copy-start(f32[32]{0:T(128)} %param.14) | copy-start | bytes 388
  15.1 15.3 %copy-start.8 = (f32[32]{0:T(128)S(1)}, f32[32]{0:T(128)}, u32[]{:S(2)}) copy-start(f32[32]{0:T(128)} %param.13) | copy-start | bytes 388
  16.2 272.6 %all-gather.4.cloned.1.call-start = ((), (), s32[]{:S(2)}) async-start(), calls=%async_computation.1 | async-start | bytes 9437184 | tf_op jit(solution)/shard_map/all_gather | solution.py:77
  24.4 66.8 %collective-permute-start = (f32[4,32,8,1,256]{4,2,3,1,0:T(8,128)S(1)}, f32[4,32,8,1,256]{4,2,3,1,0:T(8,128)S(1)}, u32[]{:S(2)}, u32[]{:S(2)}) collective-permute-start(f32[4,32,8,1,256]{4,2,3,1,0:T(8,128)S(1)} %copy.236), channel_id=1, source_target_pairs={{0,8},{8,16},{16,24},{1,9},{9,17},{17,25},{2,10},{10,18},{18,26},{... | collective-permute-start | bytes 3145736 | tf_op jit(solution)/shard_map/ppermute | solution.py:23
  27.9 64.4 %collective-permute-start.1 = (f32[4,32,8,1,256]{4,2,3,1,0:T(8,128)}, f32[4,32,8,1,256]{4,2,3,1,0:T(8,128)}, u32[]{:S(2)}, u32[]{:S(2)}) collective-permute-start(f32[4,32,8,1,256]{4,2,3,1,0:T(8,128)} %copy.238), channel_id=1, source_target_pairs={{8,0},{16,8},{24,16},{9,1},{17,9},{25,17},{10,2},{18,10},{26,18},{... | collective-permute-start | bytes 3145736 | tf_op jit(solution)/shard_map/ppermute | solution.py:26
  143.2 3.4 copy-start.2
  146.5 12.1 %copy-start.3 = (f32[2,32,1,16,256]{4,3,2,1,0:T(8,128)S(1)}, f32[2,32,1,16,256]{4,3,2,1,0:T(8,128)}, u32[]{:S(2)}) copy-start(f32[2,32,1,16,256]{4,3,2,1,0:T(8,128)} %get-tuple-element.21) | copy-start | bytes 3145732
  159.8 8.6 %copy-start.6 = (s32[1024]{0:T(1024)S(1)}, s32[1024]{0:T(1024)}, u32[]{:S(2)}) copy-start(s32[1024]{0:T(1024)} %param.17) | copy-start | bytes 12292
  165.0 351.5 %all-gather.6.cloned.1.call-start = ((), (), s32[]{:S(2)}) async-start(), calls=%async_computation.2 | async-start | bytes 1179648 | tf_op jit(solution)/shard_map/all_gather | solution.py:11
  459.6 7.1 %slice-start = ((s8[8388608]{0:T(1024)(128)(4,1)}), s8[4194304]{0:T(1024)(128)(4,1)S(1)}, s32[]{:S(2)}) async-start(s8[8388608]{0:T(1024)(128)(4,1)} %bitcast.70), calls=%async_computation.3 | async-start | bytes 8388608
  463.1 3.6 slice-start.1
  466.7 2.2 slice-start.2
  467.0 3.3 slice-start.3
  470.2 48.3 %copy-start.1 = (f32[3,32]{1,0:T(4,128)S(1)}, f32[3,32]{1,0:T(4,128)}, u32[]{:S(2)}) copy-start(f32[3,32]{1,0:T(4,128)} %param.11) | copy-start | bytes 1156
Sparse Core Ops, SparseCore 0:
  16.3 73.2 all-reduce.2
  165.2 123.5 all-gather.3
  478.3 38.2 all-gather.5
